TPU v7x, 32 devices: a whole 2x2x4 slice. The times are simulated.
32 devices in a mesh: slab: 16 (over z, y, core), amp: 2 (over x).
Axes of the slice: x: 2, y: 2, z: 4, core: 2. Of those that a mesh axis runs over, the one named last changes fastest.
Arguments:
- amplitudes: bfloat16 [409600, 704], P('slab', 'amp'), may hold values from -6 to 6
- integrals: bfloat16 [409600, 1280], P(('slab', 'amp')), may hold values from -0.0546875 to 0.0546875
- virt_irrep: int32 [640], replicated, may hold values from 0 to 7
- occ_irrep: int32 [64], replicated, may hold values from 0 to 7
Outputs:
- ladder_residual: float32 [704, 1280], P('amp', 'slab')
All inputs are finite; a program needn't handle non-finite values.
Results may differ from a plain program's by a relative error of at most 0.0003.
Values may be sent and summed in bfloat16 or wider, within the bound.
A program may use at most 128 MiB of HBM per device.

v0:
```python
import jax
import jax.numpy as jnp
from jax import lax
from jax.sharding import PartitionSpec as P


def pair_irreps(table, first, count):
    width = table.shape[0]
    base = first // width
    offset = first % width
    span = count // width + 2
    tiled = jnp.tile(table, span)
    second = lax.dynamic_slice_in_dim(tiled, offset, count)
    padded = jnp.concatenate([table, jnp.zeros((span,), jnp.int32)])
    nearby = lax.dynamic_slice_in_dim(padded, base, span)
    relative = (offset + jnp.arange(count, dtype=jnp.int32)) // width
    chosen = relative[:, None] == jnp.arange(span, dtype=jnp.int32)[None, :]
    leading = jnp.sum(jnp.where(chosen, nearby[None, :], 0), axis=1)
    return jnp.bitwise_xor(leading, second)


def contract_rows(left, right):
    return lax.dot_general(
        left, right, (((0,), (0,)), ((), ())), preferred_element_type=jnp.float32
    )


def transpose_pairs(amplitudes):
    return lax.all_to_all(amplitudes, "amp", split_axis=0, concat_axis=1, tiled=True)


def per_device(amplitudes, integrals, virt_irrep, occ_irrep):
    slab_count = lax.axis_size("slab")
    amp_count = lax.axis_size("amp")
    slab_index = lax.axis_index("slab")
    amp_index = lax.axis_index("amp")
    pair_rows = integrals.shape[0]
    columns = integrals.shape[1]
    pairs_local = amplitudes.shape[1]
    occupied = occ_irrep.shape[0]
    window_i = pairs_local * amp_count // occupied
    window_a = columns // virt_irrep.shape[0]
    owned = columns // slab_count
    column_sym = jnp.bitwise_xor(
        jnp.repeat(virt_irrep[:window_a], virt_irrep.shape[0]), jnp.tile(virt_irrep, window_a)
    )
    pair_sym = pair_irreps(
        virt_irrep, (slab_index * amp_count + amp_index) * pair_rows, integrals.shape[0]
    )
    keep = (pair_sym[:, None] == column_sym[None, :]).astype(integrals.dtype)
    kept_local = integrals * keep
    moved = transpose_pairs(amplitudes)
    mine = lax.psum_scatter(
        contract_rows(moved, kept_local), "amp", scatter_dimension=0, tiled=True
    )
    block = lax.psum_scatter(mine, "slab", scatter_dimension=1, tiled=True)
    row_sym_all = jnp.bitwise_xor(
        jnp.repeat(occ_irrep[:window_i], occupied), jnp.tile(occ_irrep, window_i)
    )
    row_sym = lax.dynamic_slice_in_dim(row_sym_all, amp_index * pairs_local, pairs_local)
    owned_sym = lax.dynamic_slice_in_dim(column_sym, slab_index * owned, owned)
    same = (row_sym[:, None] == owned_sym[None, :]).astype(jnp.float32)
    return block * same


def solution(mesh):
    return jax.shard_map(
        per_device,
        mesh=mesh,
        in_specs=(P("slab", "amp"), P(("slab", "amp"), None), P(), P()),
        out_specs=P("amp", "slab"),
        check_vma=False,
    )
```

profile of v0, /device:TPU:0, one launch (start us, length us, event | category | flops | bytes accessed | tf_op | source)
XLA Modules:
  0.0 385.8 jit_solution(203618613026039317)
XLA Ops:
  6.5 15.7 %copy.17 = bf16[44,2,8,12800]{3,2,0,1:T(8,128)(2,1)} copy(bf16[44,2,8,12800]{3,2,1,0:T(8,128)(2,1)} %bitcast.14) | data formatting | bytes 36044800 | tf_op jit(solution)/shard_map/all_to_all | solution.py:29
  22.2 0.0 copy-start
  22.2 0.0 slice-start
  22.2 10.3 %all-to-all-start = ((bf16[2,12800,352]{1,2,0:T(8,128)(2,1)}), bf16[2,12800,352]{1,2,0:T(8,128)(2,1)}, u32[]{:S(2)}, u32[]{:S(2)}) async-start(bf16[2,12800,352]{1,2,0:T(8,128)(2,1)} %bitcast.13), calls=%async_computation | async-start | bytes 36044800 | tf_op jit(solution)/shard_map/all_to_all | solution.py:29
  32.5 0.0 reduce-scatter.5.cloned.1.call-start
  32.6 0.0 copy-done
  32.6 0.0 slice-done
  32.6 0.1 broadcast_xor_fusion.1
  32.7 0.1 pad_dynamic-slice_fusion
  32.8 0.3 select_reduce_fusion
  33.2 0.1 dynamic-slice_xor_fusion
  33.3 196.3 %all-to-all-done = bf16[2,12800,352]{1,2,0:T(8,128)(2,1)} async-done(((bf16[2,12800,352]{1,2,0:T(8,128)(2,1)}), bf16[2,12800,352]{1,2,0:T(8,128)(2,1)}, u32[]{:S(2)}, u32[]{:S(2)}) %all-to-all-start) | async-done | bytes 18022432 | tf_op jit(solution)/shard_map/all_to_all | solution.py:29
  229.6 0.0 copy-start.1
  229.6 33.1 %fusion.4 = f32[704,1280]{1,0:T(8,128)} fusion(bf16[12800,704]{0,1:T(8,128)(2,1)} %bitcast.1, bf16[12800,1280]{1,0:T(8,128)(2,1)} %param.5, s32[1280]{0:T(1024)S(1)} %xor.22, s32[12800]{0:T(1024)S(1)} %dynamic-slice_xor_fusion), kind=kOutput, calls=%fused_computation.6 | convolution fusion | flops 23101440000 | bytes 54451200 | tf_op jit(solution)/shard_map/dot_general | solution.py:23
  262.7 0.0 reduce-scatter.5.cloned.1.call-update
  262.7 0.0 reduce-scatter.7.cloned.1.call-start
  262.8 49.1 %reduce-scatter.5.cloned.1.call-done = f32[352,1280]{1,0:T(8,128)} async-done(((f32[704,1280]{1,0:T(8,128)}), f32[352,1280]{1,0:T(8,128)}) %reduce-scatter.5.cloned.1.call-update) | async-done | bytes 1802256 | tf_op jit(solution)/shard_map/reduce_scatter | solution.py:53
  311.9 2.9 copy.13
  314.7 0.0 reduce-scatter.7.cloned.1.call-update
  314.8 0.1 dynamic_slice.13
  314.9 0.0 copy-done.1
  314.9 0.1 broadcast_xor_fusion
  314.9 0.1 xor.20
  315.0 0.1 dynamic_slice.12
  315.1 62.0 %reduce-scatter.7.cloned.1.call-done = f32[80,352]{1,0:T(8,128)} async-done(((f32[1280,352]{1,0:T(8,128)}), f32[80,352]{1,0:T(8,128)}) %reduce-scatter.7.cloned.1.call-update) | async-done | bytes 112656
  377.0 1.0 copy.14
  378.1 0.1 compare_select_fusion.4
  378.2 0.8 copy.12
  (4 shorter events, 0.1 us)
Async XLA Ops:
  22.2 10.4 %copy-start = (s32[640]{0:T(1024)S(1)}, s32[640]{0:T(1024)}, u32[]{:S(2)}) copy-start(s32[640]{0:T(1024)} %param.6) | copy-start | bytes 7684
  22.2 10.4 %slice-start = ((s32[640]{0:T(1024)}), s32[2]{0:T(128)S(1)}, s32[]{:S(2)}) async-start(s32[640]{0:T(1024)} %param.6), calls=%async_computation.5 | async-start | bytes 1024 | tf_op jit(solution)/shard_map/slice | solution.py:45
  22.2 207.4 %all-to-all-start = ((bf16[2,12800,352]{1,2,0:T(8,128)(2,1)}), bf16[2,12800,352]{1,2,0:T(8,128)(2,1)}, u32[]{:S(2)}, u32[]{:S(2)}) async-start(bf16[2,12800,352]{1,2,0:T(8,128)(2,1)} %bitcast.13), calls=%async_computation | async-start | bytes 36044800 | tf_op jit(solution)/shard_map/all_to_all | solution.py:29
  32.5 279.4 %reduce-scatter.5.cloned.1.call-start = ((), (), s32[]{:S(2)}) async-start(), calls=%async_computation.3 | async-start | bytes 5406720 | tf_op jit(solution)/shard_map/reduce_scatter | solution.py:53
  229.6 85.3 %copy-start.1 = (s32[64]{0:T(128)S(1)}, s32[64]{0:T(128)}, u32[]{:S(2)}) copy-start(s32[64]{0:T(128)} %param.7) | copy-start | bytes 772
  262.7 114.3 %reduce-scatter.7.cloned.1.call-start = ((), (), s32[]{:S(2)}) async-start(), calls=%async_computation.4 | async-start | bytes 2088960
Sparse Core Ops, SparseCore 0:
  262.9 48.9 reduce-scatter.4
  315.6 61.3 reduce-scatter.6
where the time goes:
time: 386 us
  waiting for transfers between devices  307 us (80%)
  matrix products  33.1 us (9%)
  local copies, waits for them, and re-layouts  20.6 us (5%)
  between operations  13.5 us (3%)
  starting transfers between devices  10.4 us (3%)
    all_to_all x1, waiting for transfers between devices, transpose_pairs(): lax.all_to_all(amplitudes, 'amp', split_axis=0, concat_axis=1, tiled=True)  196 us
    unnamed x3, waiting for transfers between devices  62 us
    reduce_scatter x1, waiting for transfers between devices, per_device(): lax.psum_scatter(contract_rows(moved, kept_local), 'amp', scatter_dimensi...  49.1 us
    dot_general x1, matrix products, contract_rows(): lax.dot_general(left, right, (((0,), (0,)), ((), ())), preferred_element_...  33.1 us
    all_to_all x1, local copies, waits for them, and re-layouts, transpose_pairs(): lax.all_to_all(amplitudes, 'amp', split_axis=0, concat_axis=1, tiled=True)  15.7 us
    all_to_all x1, starting transfers between devices, transpose_pairs(): lax.all_to_all(amplitudes, 'amp', split_axis=0, concat_axis=1, tiled=True)  10.3 us
  transfers between devices with their start and end apart: 3, of which 3 were waited for; matrix products, arithmetic and copies ran while one was open for 0% of the time, Pallas kernels for 0%

commit v1 on v0

v1 whole, which is shorter than its diff:
```python
import functools
import math

import jax
import jax.numpy as jnp
from jax import lax
from jax.experimental import pallas as pl
from jax.experimental.pallas import tpu as pltpu
from jax.sharding import PartitionSpec as P

MESH = pl.DeviceIdType.MESH
AMP_SLOTS = 6
INT_SLOTS = 6


def contract_kernel(slabs, amps, virt_count, amp_ref, int_ref, pick_ref, row_sym_ref, col_sym_ref,
                    virt_lanes_ref, virt_ref, out_ref, amp_buf, int_buf, sent, packed,
                    amp_sem, int_sem, send_sem, recv_sem):
    slab = lax.axis_index("slab")
    me = lax.axis_index("amp")
    blocks, cap, block = sent.shape[1], sent.shape[2], sent.shape[3]
    pair_rows = blocks * block
    width = 256

    def amp_copy(step):
        owner = lax.rem(me + 1 + step // blocks, amps)
        start = owner * pair_rows + lax.rem(step, blocks) * block
        slot = lax.rem(step, AMP_SLOTS)
        return pltpu.make_async_copy(
            amp_ref.at[pl.ds(pl.multiple_of(start, 32), block)], amp_buf.at[slot], amp_sem.at[slot])

    def int_copy(step):
        slot = lax.rem(step, INT_SLOTS)
        return pltpu.make_async_copy(
            int_ref.at[pl.ds(pl.multiple_of(step * block, 32), block)], int_buf.at[slot], int_sem.at[slot])

    steps = blocks * amps
    for step in range(min(AMP_SLOTS, steps)):
        amp_copy(jnp.int32(step)).start()
    for step in range(min(INT_SLOTS, blocks)):
        int_copy(jnp.int32(step)).start()

    if amps > 1:
        barrier = pltpu.get_barrier_semaphore()
        for hop in range(1, amps):
            pl.semaphore_signal(barrier, inc=1, device_id=(slab, lax.rem(me + hop, amps)), device_id_type=MESH)
        pl.semaphore_wait(barrier, amps - 1)

    def first_of(owner, index):
        row = (slab * amps + owner) * pair_rows + index * block
        return row // virt_count, lax.rem(row, virt_count)

    def compact(step):
        owner = lax.rem(me + 1 + step // blocks, amps)
        index = lax.rem(step, blocks)
        lead, offset = first_of(owner, index)
        slot = lax.rem(step, AMP_SLOTS)
        amp_copy(step).wait()
        second = virt_lanes_ref[pl.ds(pl.multiple_of(offset, 32), block), :]
        wanted = jnp.bitwise_xor(row_sym_ref[...], virt_ref[lead]).astype(jnp.bfloat16)
        columns = amp_buf.shape[2]
        parts = []
        for begin in range(0, columns, 128):
            end = min(begin + 128, columns)
            piece = amp_buf[slot, :, begin:end]
            parts.append(jnp.where(second[:, : end - begin] == wanted[:, begin:end], piece, jnp.zeros_like(piece)))
        masked = jnp.concatenate(parts, axis=1) if len(parts) > 1 else parts[0]
        return index, lax.dot_general(
            pick_ref[...], masked, (((1,), (1,)), ((), ())), preferred_element_type=jnp.float32
        ).astype(jnp.bfloat16)

    def refill(step):
        @pl.when(step + AMP_SLOTS < steps)
        def _():
            amp_copy(step + AMP_SLOTS).start()

    def remote(hop, index):
        return pltpu.make_async_remote_copy(
            src_ref=sent.at[hop, index],
            dst_ref=packed.at[index, pl.ds(pl.multiple_of(me * cap, 16), cap)],
            send_sem=send_sem.at[hop, index],
            recv_sem=recv_sem.at[hop, index],
            device_id=(slab, lax.rem(me + 1 + hop, amps)),
            device_id_type=MESH)

    def send_step(step, carry):
        index, block_of = compact(step)
        hop = step // blocks
        sent[hop, index] = block_of
        remote(hop, index).start()
        refill(step)
        return carry

    lax.fori_loop(0, steps - blocks, send_step, 0)

    def own_step(step, carry):
        index, block_of = compact(step)
        packed[index, pl.ds(pl.multiple_of(me * cap, 16), cap), :] = block_of
        refill(step)
        return carry

    lax.fori_loop(steps - blocks, steps, own_step, 0)

    out_ref[...] = jnp.zeros_like(out_ref)

    def contract(index, carry):
        slot = lax.rem(index, INT_SLOTS)
        lead, offset = first_of(me, index)
        int_copy(index).wait()
        for hop in range(amps - 1):
            remote(hop, index).wait_recv()
        second = virt_lanes_ref[pl.ds(pl.multiple_of(offset, 32), block), :]
        wanted = jnp.bitwise_xor(col_sym_ref[...], virt_ref[lead]).astype(jnp.bfloat16)
        left = packed[index]
        for begin in range(0, out_ref.shape[1], width):
            parts = []
            for at in range(begin, begin + width, 128):
                piece = int_buf[slot, :, at:at + 128]
                parts.append(jnp.where(second == wanted[:, at:at + 128], piece, jnp.zeros_like(piece)))
            out_ref[:, begin:begin + width] += jnp.dot(
                left, jnp.concatenate(parts, axis=1), preferred_element_type=jnp.float32)

        @pl.when(index + INT_SLOTS < blocks)
        def _():
            int_copy(index + INT_SLOTS).start()
        return carry

    lax.fori_loop(0, blocks, contract, 0)

    def drain(step, carry):
        remote(step // blocks, lax.rem(step, blocks)).wait_send()
        return carry

    lax.fori_loop(0, steps - blocks, drain, 0)


def contract_pairs(amplitudes, integrals, pick, row_sym, col_sym, virt_lanes, virt_irrep):
    slabs = lax.axis_size("slab")
    amps = lax.axis_size("amp")
    cap = pick.shape[0]
    virt_count = virt_irrep.shape[0]
    pair_rows, columns = integrals.shape
    block = math.gcd(pair_rows, virt_count)
    blocks = pair_rows // block
    hops = max(amps - 1, 1)
    vmem = pl.BlockSpec(memory_space=pltpu.VMEM)
    return pl.pallas_call(
        functools.partial(contract_kernel, slabs, amps, virt_count),
        out_shape=jax.ShapeDtypeStruct((amps * cap, columns), jnp.float32),
        in_specs=[pl.BlockSpec(memory_space=pltpu.HBM)] * 2 + [vmem] * 4
        + [pl.BlockSpec(memory_space=pltpu.SMEM)],
        out_specs=vmem,
        scratch_shapes=[
            pltpu.VMEM((AMP_SLOTS, block, amplitudes.shape[1]), jnp.bfloat16),
            pltpu.VMEM((INT_SLOTS, block, columns), jnp.bfloat16),
            pltpu.VMEM((hops, blocks, cap, block), jnp.bfloat16),
            pltpu.VMEM((blocks, amps * cap, block), jnp.bfloat16),
            pltpu.SemaphoreType.DMA((AMP_SLOTS,)),
            pltpu.SemaphoreType.DMA((INT_SLOTS,)),
            pltpu.SemaphoreType.DMA((hops, blocks)),
            pltpu.SemaphoreType.DMA((hops, blocks)),
        ],
        compiler_params=pltpu.CompilerParams(
            collective_id=0, has_side_effects=True, vmem_limit_bytes=56 * 1024 * 1024),
    )(amplitudes, integrals, pick, row_sym, col_sym, virt_lanes, virt_irrep)


def per_device(amplitudes, integrals, virt_irrep, occ_irrep):
    slab_count = lax.axis_size("slab")
    amp_count = lax.axis_size("amp")
    slab_index = lax.axis_index("slab")
    amp_index = lax.axis_index("amp")
    columns = integrals.shape[1]
    pairs_local = amplitudes.shape[1]
    occupied = occ_irrep.shape[0]
    virt_count = virt_irrep.shape[0]
    window_i = pairs_local * amp_count // occupied
    window_a = columns // virt_count
    owned = columns // slab_count
    cap = max(16, pairs_local * 3 // 256 * 16)

    column_sym = jnp.bitwise_xor(
        jnp.repeat(virt_irrep[:window_a], virt_count), jnp.tile(virt_irrep, window_a))
    row_sym_all = jnp.bitwise_xor(
        jnp.repeat(occ_irrep[:window_i], occupied), jnp.tile(occ_irrep, window_i)
    ).reshape(amp_count, pairs_local)
    position = jnp.arange(pairs_local)
    alike = (row_sym_all[:, :, None] == row_sym_all[:, None, :]) & (position[:, None] > position[None, :])
    rank_all = jnp.sum(alike, axis=2, dtype=jnp.int32)
    passes = jnp.max(rank_all) // cap + 1
    row_sym = lax.dynamic_index_in_dim(row_sym_all, amp_index, 0, keepdims=False)
    rank = lax.dynamic_index_in_dim(rank_all, amp_index, 0, keepdims=False)
    owned_sym = lax.dynamic_slice_in_dim(column_sym, slab_index * owned, owned)
    same = row_sym[:, None] == owned_sym[None, :]
    virt_lanes = jnp.broadcast_to(virt_irrep.astype(jnp.bfloat16)[:, None], (virt_count, 128))

    def one_pass(turn, total):
        chosen = rank[None, :] - turn * cap == jnp.arange(cap)[:, None]
        part = contract_pairs(
            amplitudes, integrals, chosen.astype(jnp.bfloat16), row_sym[None, :], column_sym[None, :],
            virt_lanes, virt_irrep)
        part = lax.psum_scatter(part, "amp", scatter_dimension=0, tiled=True)
        part = lax.psum_scatter(part, "slab", scatter_dimension=1, tiled=True)
        spread = lax.dot_general(
            chosen.astype(jnp.float32), part, (((0,), (0,)), ((), ())),
            precision=lax.Precision.HIGHEST, preferred_element_type=jnp.float32)
        return total + jnp.where(same, spread, 0.0)

    return lax.fori_loop(0, passes, one_pass, jnp.zeros((pairs_local, owned), jnp.float32))


def solution(mesh):
    return jax.shard_map(
        per_device,
        mesh=mesh,
        in_specs=(P("slab", "amp"), P(("slab", "amp"), None), P(), P()),
        out_specs=P("amp", "slab"),
        check_vma=False,
    )
```

time: 386 us -> 171 us (0.44)
  waiting for transfers between devices: 307 us -> 74.6 us
  Pallas kernels: 0 us -> 43.8 us
  matrix products: 33.1 us -> 1 us
  starting transfers between devices: 10.4 us -> 0.08 us
  local copies, waits for them, and re-layouts: 20.6 us -> 30.4 us
    all_to_all x1 -> x0, waiting for transfers between devices: 196 us -> none  [transpose_pairs(): lax.all_to_all(amplitudes, 'amp', split_axis=0, concat_axis=1, tiled=True)]
    unnamed x3 -> x0, waiting for transfers between devices: 62 us -> none
    while x0 -> x3, waiting for transfers between devices: none -> 58.1 us
    pallas_call x0 -> x1, Pallas kernels: none -> 43.8 us  [contract_pairs(): pl.pallas_call(functools.partial(contract_kernel, slabs, amps, virt_count...]
    reduce_scatter x1, waiting for transfers between devices: 49.1 us -> 16.5 us  [one_pass(): part = lax.psum_scatter(part, 'amp', scatter_dimension=0, tiled=True)]
    dot_general x1, matrix products: 33.1 us -> 1 us  [one_pass(): lax.dot_general(chosen.astype(jnp.float32), part, (((0,), (0,)), ((), ())...]
    unnamed x6 -> x5, local copies, waits for them, and re-layouts: 3.88 us -> 26.1 us
    all_to_all x1 -> x0, local copies, waits for them, and re-layouts: 15.7 us -> none  [transpose_pairs(): lax.all_to_all(amplitudes, 'amp', split_axis=0, concat_axis=1, tiled=True)]
  transfers between devices with their start and end apart: 3 -> 2, of which waited for: 3 -> 2; matrix products, arithmetic and copies ran while one was open for 0% -> 0% of each run, Pallas kernels for 0% -> 0%
where the time goes in v1:
time: 171 us; the launch traced here: 170 us
  waiting for transfers between devices  74.6 us (44%)
  Pallas kernels  43.8 us (26%)
  local copies, waits for them, and re-layouts  30.4 us (18%)
  between operations  16 us (9%)
  other arithmetic  4.03 us (2%)
    while x3, waiting for transfers between devices  58.1 us
    pallas_call x1, Pallas kernels, contract_pairs(): pl.pallas_call(functools.partial(contract_kernel, slabs, amps, virt_count...  43.8 us
    unnamed x5, local copies, waits for them, and re-layouts  26.1 us
    reduce_scatter x1, waiting for transfers between devices, one_pass(): part = lax.psum_scatter(part, 'amp', scatter_dimension=0, tiled=True)  16.5 us
  transfers between devices with their start and end apart: 2, of which 2 were waited for; matrix products, arithmetic and copies ran while one was open for 0% of the time, Pallas kernels for 0%

profile of v1, /device:TPU:0, one launch (start us, length us, event | category | flops | bytes accessed | tf_op | source)
XLA Modules:
  0.0 170.0 jit_solution(17380161800969693187)
XLA Ops:
  6.5 0.7 slice.7
  7.2 0.7 convert_element_type.11
  7.9 0.8 broadcast_xor_fusion.1
  8.7 0.1 dynamic_slice.12
  8.8 0.8 broadcast_xor_fusion
  9.6 0.1 xor.22
  9.7 0.4 convert_reduce_fusion
  10.1 0.6 reduce_max.9
  13.4 0.0 copy-start.1
  13.4 25.4 %copy.7 = bf16[25600,352]{1,0:T(8,128)(2,1)} copy(bf16[25600,352]{0,1:T(8,128)(2,1)} %param.6) | data formatting | bytes 36044800
  38.8 0.0 copy-done.1
  38.8 123.7 %while.13 = (s32[]{:T(128)}, f32[352,80]{0,1:T(8,128)S(1)}, s32[]{:T(128)}, s32[352]{0:T(512)S(1)}, s32[352]{0:T(512)S(1)}, /*index=5*/bf16[25600,352]{1,0:T(8,1...) while((s32[]{:T(128)}, f32[352,80]{0,1:T(8,128)S(1)}, ...), condition=%wide.wide.region_5.6_spmd.clone.clone, body=%wide.wide.region_2.5_spmd.clone.clone.sunk | while | flops 21780580 | bytes 5478573 | solution.py:209
  38.8 0.0 reduce-scatter.8.cloned.1.call-start
  38.9 0.1 xor_bitcast_fusion.3
  39.0 0.6 copy.15
  39.6 0.6 fusion.17.pick_ref
  40.2 0.8 broadcast_in_dim.66.virt_lanes_ref
  41.0 43.8 %body.1 = f32[128,1280]{1,0:T(8,128)} custom-call(bf16[25600,352]{1,0:T(8,128)(2,1)} %get-tuple-element.340.amp_ref, bf16[12800,1280]{1,0:T(8,128)(2,1)} %get-tuple-element.341.int_ref, bf16[64,352]{1,0:T(8,128)(2,1)} %fusion.17.pick_ref, s32[1,352]{1,0:T(1,128)S(1)} %get-tuple-element.346.row_sym_ref, s32[1,1280]{1,0:T(1,128)} %bitcast.22, ...), custom_call_target="tpu_custom_call" | custom-call | tf_op jit(solution)/shard_map/while/body/pallas_call | solution.py:147
  84.8 0.0 reduce-scatter.8.cloned.1.call-update
  84.9 0.0 reduce-scatter.10.cloned.1.call-start
  84.9 16.5 %reduce-scatter.8.cloned.1.call-done = f32[64,1280]{1,0:T(8,128)} async-done(((f32[128,1280]{1,0:T(8,128)}), f32[64,1280]{1,0:T(8,128)}) %reduce-scatter.8.cloned.1.call-update) | async-done | bytes 327696 | tf_op jit(solution)/shard_map/while/body/reduce_scatter | solution.py:202
  101.4 2.1 %copy.16 = f32[64,1280]{0,1:T(8,128)} copy(f32[64,1280]{1,0:T(8,128)} %reduce-scatter.8.cloned.1.call-done) | data formatting | bytes 655360 | tf_op jit(solution)/shard_map/while
  103.5 0.0 reduce-scatter.10.cloned.1.call-update
  103.5 58.0 %reduce-scatter.10.cloned.1.call-done = f32[80,64]{1,0:T(8,128)} async-done(((f32[1280,64]{1,0:T(8,128)}), f32[80,64]{1,0:T(8,128)}) %reduce-scatter.10.cloned.1.call-update) | async-done | bytes 20496 | tf_op jit(solution)/shard_map/while
  161.5 1.0 fusion.18
  162.5 0.0 copy-start
  162.5 0.6 copy-done
  (6 shorter events, 0.1 us)
Async XLA Ops:
  13.4 25.5 %copy-start.1 = (s32[640]{0:T(1024)S(1)}, s32[640]{0:T(1024)}, u32[]{:S(2)}) copy-start(s32[640]{0:T(1024)} %param.8) | copy-start | bytes 7684
  38.8 62.5 %reduce-scatter.8.cloned.1.call-start = ((), (), s32[]{:S(2)}) async-start(), calls=%async_computation.2 | async-start | bytes 983040 | tf_op jit(solution)/shard_map/while/body/reduce_scatter | solution.py:202
  84.9 76.7 %reduce-scatter.10.cloned.1.call-start = ((), (), s32[]{:S(2)}) async-start(), calls=%async_computation.3 | async-start | bytes 696320 | tf_op jit(solution)/shard_map/while
  162.5 0.7 copy-start
Sparse Core Ops, SparseCore 0:
  85.0 16.3 reduce-scatter.7
  104.9 56.5 reduce-scatter.9

commit v2 on v1

--- a/solution.py
+++ b/solution.py
@@ -13,21 +13,34 @@
 INT_SLOTS = 6
 
 
-def contract_kernel(slabs, amps, virt_count, amp_ref, int_ref, pick_ref, row_sym_ref, col_sym_ref,
-                    virt_lanes_ref, virt_ref, out_ref, amp_buf, int_buf, sent, packed,
-                    amp_sem, int_sem, send_sem, recv_sem):
+def bit_reversed(index, bits):
+    return int(format(index, "b").zfill(bits)[::-1], 2) if bits else 0
+
+
+def contract_kernel(slabs, amps, virt_count, turned, amp_ref, int_ref, pick_ref, row_sym_ref, col_sym_ref,
+                    virt_lanes_ref, virt_row_ref, virt_ref, out_ref, amp_buf, int_buf, sent, packed, acc,
+                    halves, arrived, last_in, amp_sem, int_sem, send_sem, recv_sem,
+                    half_send, half_recv, last_send, last_recv):
     slab = lax.axis_index("slab")
     me = lax.axis_index("amp")
     blocks, cap, block = sent.shape[1], sent.shape[2], sent.shape[3]
     pair_rows = blocks * block
     width = 256
+    bits = slabs.bit_length() - 1
+    owned = halves.shape[1]
+
+    def slab_partner(bit):
+        return slab + (1 << bit) - 2 * (1 << bit) * lax.rem(slab // (1 << bit), 2)
 
     def amp_copy(step):
         owner = lax.rem(me + 1 + step // blocks, amps)
         start = owner * pair_rows + lax.rem(step, blocks) * block
         slot = lax.rem(step, AMP_SLOTS)
-        return pltpu.make_async_copy(
-            amp_ref.at[pl.ds(pl.multiple_of(start, 32), block)], amp_buf.at[slot], amp_sem.at[slot])
+        if turned:
+            source = amp_ref.at[:, pl.ds(pl.multiple_of(start, 128), block)]
+        else:
+            source = amp_ref.at[pl.ds(pl.multiple_of(start, 32), block)]
+        return pltpu.make_async_copy(source, amp_buf.at[slot], amp_sem.at[slot])
 
     def int_copy(step):
         slot = lax.rem(step, INT_SLOTS)
@@ -40,11 +53,12 @@
     for step in range(min(INT_SLOTS, blocks)):
         int_copy(jnp.int32(step)).start()
 
-    if amps > 1:
-        barrier = pltpu.get_barrier_semaphore()
-        for hop in range(1, amps):
-            pl.semaphore_signal(barrier, inc=1, device_id=(slab, lax.rem(me + hop, amps)), device_id_type=MESH)
-        pl.semaphore_wait(barrier, amps - 1)
+    barrier = pltpu.get_barrier_semaphore()
+    for hop in range(1, amps):
+        pl.semaphore_signal(barrier, inc=1, device_id=(slab, lax.rem(me + hop, amps)), device_id_type=MESH)
+    for bit in range(bits):
+        pl.semaphore_signal(barrier, inc=1, device_id=(slab_partner(bit), me), device_id_type=MESH)
+    pl.semaphore_wait(barrier, amps - 1 + bits)
 
     def first_of(owner, index):
         row = (slab * amps + owner) * pair_rows + index * block
@@ -56,6 +70,16 @@
         lead, offset = first_of(owner, index)
         slot = lax.rem(step, AMP_SLOTS)
         amp_copy(step).wait()
+        if turned:
+            second = virt_row_ref[:, pl.ds(pl.multiple_of(offset, 128), block)]
+            held = jnp.bitwise_xor(second, virt_ref[lead]).astype(jnp.bfloat16)
+            parts = []
+            for begin in range(0, block, 128):
+                piece = amp_buf[slot, :, begin:begin + 128]
+                parts.append(jnp.where(row_sym_ref[...] == held[:, begin:begin + 128], piece, jnp.zeros_like(piece)))
+            return index, jnp.dot(
+                pick_ref[...], jnp.concatenate(parts, axis=1), preferred_element_type=jnp.float32
+            ).astype(jnp.bfloat16)
         second = virt_lanes_ref[pl.ds(pl.multiple_of(offset, 32), block), :]
         wanted = jnp.bitwise_xor(row_sym_ref[...], virt_ref[lead]).astype(jnp.bfloat16)
         columns = amp_buf.shape[2]
@@ -101,7 +125,7 @@
 
     lax.fori_loop(steps - blocks, steps, own_step, 0)
 
-    out_ref[...] = jnp.zeros_like(out_ref)
+    acc[...] = jnp.zeros_like(acc)
 
     def contract(index, carry):
         slot = lax.rem(index, INT_SLOTS)
@@ -112,12 +136,12 @@
         second = virt_lanes_ref[pl.ds(pl.multiple_of(offset, 32), block), :]
         wanted = jnp.bitwise_xor(col_sym_ref[...], virt_ref[lead]).astype(jnp.bfloat16)
         left = packed[index]
-        for begin in range(0, out_ref.shape[1], width):
+        for begin in range(0, acc.shape[1], width):
             parts = []
             for at in range(begin, begin + width, 128):
                 piece = int_buf[slot, :, at:at + 128]
                 parts.append(jnp.where(second == wanted[:, at:at + 128], piece, jnp.zeros_like(piece)))
-            out_ref[:, begin:begin + width] += jnp.dot(
+            acc[:, begin:begin + width] += jnp.dot(
                 left, jnp.concatenate(parts, axis=1), preferred_element_type=jnp.float32)
 
         @pl.when(index + INT_SLOTS < blocks)
@@ -126,6 +150,50 @@
         return carry
 
     lax.fori_loop(0, blocks, contract, 0)
+
+    for owner in range(slabs):
+        halves[bit_reversed(owner, bits)] = acc[:, owner * owned:(owner + 1) * owned].T
+
+    base = jnp.int32(0)
+    started = []
+    filled = 0
+    for bit in range(bits):
+        count = slabs >> (bit + 1)
+        mine = lax.rem(slab // (1 << bit), 2)
+        keep = base + mine * count
+        leave = base + (1 - mine) * count
+        copy = pltpu.make_async_remote_copy(
+            src_ref=halves.at[pl.ds(leave, count)],
+            dst_ref=arrived.at[pl.ds(filled, count)],
+            send_sem=half_send.at[bit],
+            recv_sem=half_recv.at[bit],
+            device_id=(slab_partner(bit), me),
+            device_id_type=MESH)
+        copy.start()
+        copy.wait_recv()
+        started.append(copy)
+        halves[pl.ds(keep, count)] = halves[pl.ds(keep, count)] + arrived[filled:filled + count]
+        base = keep
+        filled += count
+
+    exchanges = []
+    for hop in range(amps - 1):
+        copy = pltpu.make_async_remote_copy(
+            src_ref=halves.at[base],
+            dst_ref=last_in.at[hop],
+            send_sem=last_send.at[hop],
+            recv_sem=last_recv.at[hop],
+            device_id=(slab, lax.rem(me + 1 + hop, amps)),
+            device_id_type=MESH)
+        copy.start()
+        exchanges.append(copy)
+    total = halves[base]
+    for hop, copy in enumerate(exchanges):
+        copy.wait_recv()
+        total = total + last_in[hop]
+    out_ref[...] = total
+    for copy in started + exchanges:
+        copy.wait_send()
 
     def drain(step, carry):
         remote(step // blocks, lax.rem(step, blocks)).wait_send()
@@ -143,26 +211,43 @@
     block = math.gcd(pair_rows, virt_count)
     blocks = pair_rows // block
     hops = max(amps - 1, 1)
+    bits = slabs.bit_length() - 1
+    assert slabs == 1 << bits
+    owned = columns // slabs
+    lanes = amps * cap
+    pairs_local = amplitudes.shape[1]
+    turned = block % 128 == 0
+    if turned:
+        amplitudes = amplitudes.T
+        row_sym = jnp.broadcast_to(row_sym.astype(jnp.bfloat16).T, (pairs_local, 128))
     vmem = pl.BlockSpec(memory_space=pltpu.VMEM)
     return pl.pallas_call(
-        functools.partial(contract_kernel, slabs, amps, virt_count),
-        out_shape=jax.ShapeDtypeStruct((amps * cap, columns), jnp.float32),
-        in_specs=[pl.BlockSpec(memory_space=pltpu.HBM)] * 2 + [vmem] * 4
+        functools.partial(contract_kernel, slabs, amps, virt_count, turned),
+        out_shape=jax.ShapeDtypeStruct((owned, lanes), jnp.float32),
+        in_specs=[pl.BlockSpec(memory_space=pltpu.HBM)] * 2 + [vmem] * 5
         + [pl.BlockSpec(memory_space=pltpu.SMEM)],
         out_specs=vmem,
         scratch_shapes=[
-            pltpu.VMEM((AMP_SLOTS, block, amplitudes.shape[1]), jnp.bfloat16),
+            pltpu.VMEM((AMP_SLOTS, pairs_local, block) if turned else (AMP_SLOTS, block, pairs_local), jnp.bfloat16),
             pltpu.VMEM((INT_SLOTS, block, columns), jnp.bfloat16),
             pltpu.VMEM((hops, blocks, cap, block), jnp.bfloat16),
-            pltpu.VMEM((blocks, amps * cap, block), jnp.bfloat16),
+            pltpu.VMEM((blocks, lanes, block), jnp.bfloat16),
+            pltpu.VMEM((lanes, columns), jnp.float32),
+            pltpu.VMEM((slabs, owned, lanes), jnp.float32),
+            pltpu.VMEM((max(slabs - 1, 1), owned, lanes), jnp.float32),
+            pltpu.VMEM((hops, owned, lanes), jnp.float32),
             pltpu.SemaphoreType.DMA((AMP_SLOTS,)),
             pltpu.SemaphoreType.DMA((INT_SLOTS,)),
             pltpu.SemaphoreType.DMA((hops, blocks)),
             pltpu.SemaphoreType.DMA((hops, blocks)),
+            pltpu.SemaphoreType.DMA((max(bits, 1),)),
+            pltpu.SemaphoreType.DMA((max(bits, 1),)),
+            pltpu.SemaphoreType.DMA((hops,)),
+            pltpu.SemaphoreType.DMA((hops,)),
         ],
         compiler_params=pltpu.CompilerParams(
             collective_id=0, has_side_effects=True, vmem_limit_bytes=56 * 1024 * 1024),
-    )(amplitudes, integrals, pick, row_sym, col_sym, virt_lanes, virt_irrep)
+    )(amplitudes, integrals, pick, row_sym, col_sym, virt_lanes, virt_irrep[None, :], virt_irrep)
 
 
 def per_device(amplitudes, integrals, virt_irrep, occ_irrep):
@@ -199,10 +284,9 @@
         part = contract_pairs(
             amplitudes, integrals, chosen.astype(jnp.bfloat16), row_sym[None, :], column_sym[None, :],
             virt_lanes, virt_irrep)
-        part = lax.psum_scatter(part, "amp", scatter_dimension=0, tiled=True)
-        part = lax.psum_scatter(part, "slab", scatter_dimension=1, tiled=True)
+        part = lax.dynamic_slice_in_dim(part, amp_index * cap, cap, axis=1)
         spread = lax.dot_general(
-            chosen.astype(jnp.float32), part, (((0,), (0,)), ((), ())),
+            chosen.astype(jnp.float32), part, (((0,), (1,)), ((), ())),
             precision=lax.Precision.HIGHEST, preferred_element_type=jnp.float32)
         return total + jnp.where(same, spread, 0.0)
 

time: 171 us -> 76 us (0.44)
  waiting for transfers between devices: 74.6 us -> 0 us
  local copies, waits for them, and re-layouts: 30.4 us -> 4.35 us
  Pallas kernels: 43.8 us -> 62.7 us
  between operations: 16 us -> 2.64 us
    while x3 -> x0, waiting for transfers between devices: 58.1 us -> none
    unnamed x5 -> x2, local copies, waits for them, and re-layouts: 26.1 us -> 0.64 us
    pallas_call x1, Pallas kernels: 43.8 us -> 62.7 us  [contract_pairs(): pl.pallas_call(functools.partial(contract_kernel, slabs, amps, virt_count...]
    reduce_scatter x1 -> x0, waiting for transfers between devices: 16.5 us -> none  [one_pass(): part = lax.psum_scatter(part, 'amp', scatter_dimension=0, tiled=True)]
    while x2 -> x1, local copies, waits for them, and re-layouts: 2.65 us -> 0.6 us
  transfers between devices with their start and end apart: 2 -> 0, of which waited for: 2 -> 0; matrix products, arithmetic and copies ran while one was open for 0% -> 0% of each run, Pallas kernels for 0% -> 0%
where the time goes in v2:
time: 76 us; the launch traced here: 75.6 us
  Pallas kernels  62.7 us (82%)
  other arithmetic  4.77 us (6%)
  local copies, waits for them, and re-layouts  4.35 us (6%)
  between operations  2.64 us (3%)
  matrix products  1.07 us (1%)
    pallas_call x1, Pallas kernels, contract_pairs(): pl.pallas_call(functools.partial(contract_kernel, slabs, amps, virt_count...  62.7 us

profile of v2, /device:TPU:0, one launch (start us, length us, event | category | flops | bytes accessed | tf_op | source)
XLA Modules:
  0.0 75.6 jit_solution(2014305855403809774)
XLA Ops:
  0.0 0.7 slice.7
  0.7 0.7 convert_element_type.30
  1.4 0.7 broadcast_in_dim.72
  2.1 0.8 %broadcast_xor_fusion.1 = s32[2,640]{1,0:T(2,128)S(1)} fusion(s32[640]{0:T(1024)} %param.8, s32[2]{0:T(128)S(1)} %slice.7), kind=kLoop, calls=%fused_computation.15 | loop fusion | flops 1280 | bytes 7688 | tf_op jit(solution)/shard_map/xor | solution.py:267
  2.8 0.1 dynamic_slice.17
  2.9 0.8 %broadcast_xor_fusion = s32[11,64]{1,0:T(8,128)S(1)} fusion(s32[64]{0:T(128)} %param.9, s32[11]{0:T(128)} %bitcast.19), kind=kLoop, calls=%fused_computation.14 | loop fusion | flops 704 | bytes 3116 | tf_op jit(solution)/shard_map/xor | solution.py:269
  3.7 0.1 xor.22
  3.8 0.4 convert_reduce_fusion
  4.2 0.6 reduce_max.9
  7.5 67.4 %while.15 = (s32[]{:T(128)}, f32[352,80]{0,1:T(8,128)S(1)}, s32[]{:T(128)}, s32[352]{0:T(512)S(1)}, bf16[25600,352]{0,1:T(8,128)(2,1)}, /*index=5*/bf16[352,1]{0...) while((s32[]{:T(128)}, f32[352,80]{0,1:T(8,128)S(1)}, ...), condition=%wide.wide.region_3.4_spmd.clone.clone, body=%wide.wide.region_2.3_spmd.clone.clone.sunk | while | flops 21780580 | bytes 594107 | solution.py:293
  7.6 0.8 %xor_bitcast_fusion.3 = s32[1,1,2,640]{3,2,1,0:T(2,128)S(1)} fusion(s32[640]{0:T(1024)} %get-tuple-element.428.virt_ref, s32[2]{0:T(128)S(1)} %get-tuple-element.431), kind=kLoop, calls=%fused_computation.9.clone.clone.1 | loop fusion | flops 1280 | bytes 7688 | tf_op jit(solution)/shard_map/while
  8.3 0.6 copy.8
  8.9 0.6 fusion.18.pick_ref
  9.6 0.8 broadcast_in_dim.84.row_sym_ref
  10.3 0.8 %broadcast_in_dim.85.virt_lanes_ref = bf16[640,128]{1,0:T(8,128)(2,1)} broadcast(bf16[640]{0:T(1024)(128)(2,1)S(1)} %get-tuple-element.432), dimensions={0} | broadcast | bytes 165120 | tf_op jit(solution)/shard_map/broadcast_in_dim | solution.py:280
  11.1 62.7 %body.3 = f32[80,128]{1,0:T(8,128)} custom-call(bf16[352,25600]{1,0:T(8,128)(2,1)} %bitcast.17, bf16[12800,1280]{1,0:T(8,128)(2,1)} %get-tuple-element.429.int_ref, bf16[64,352]{1,0:T(8,128)(2,1)} %fusion.18.pick_ref, bf16[352,128]{1,0:T(8,128)(2,1)} %broadcast_in_dim.84.row_sym_ref, s32[1,1280]{1,0:T(1,128)} %bitcast.18, ...), custom_call_target="tpu_custom_call" | custom-call | tf_op jit(solution)/shard_map/while/body/pallas_call | solution.py:224
  73.9 1.1 %fusion.19 = f32[352,80]{0,1:T(8,128)S(1)} fusion(f32[352,80]{0,1:T(8,128)S(1)} %get-tuple-element.406, s32[352]{0:T(512)S(1)} %get-tuple-element.434, s32[80]{0:T(128)S(1)} %get-tuple-element.433, s32[352]{0:T(512)S(1)} %broadcast_subtract_fusion.3, f32[80,128]{1,0:T(8,128)} %body.3, s32[]{:T(128)} %get-tuple-element.430), kind=kOutput, calls=%fused_computation.4.clone.clone.1 | convolution fusion | flops 21733888 | bytes 269380 | tf_op jit(solution)/shard_map/while/body/dot_general | solution.py:288
  75.0 0.0 copy-start
  75.0 0.6 copy-done
  (6 shorter events, 0.1 us)
Async XLA Ops:
  75.0 0.7 copy-start
